TPU v7x, 32 devices: a whole 2x2x4 slice. The times are simulated.
32 devices in a mesh: comp: 4 (over y, core), gx: 2 (over x), gy: 4 (over z).
Axes of the slice: x: 2, y: 2, z: 4, core: 2. Of those that a mesh axis runs over, the one named last changes fastest.
Arguments:
- field: float32 [4, 256, 64, 256], P('comp', 'gx', 'gy'), may hold values from -6 to 6
- third_level: int32 [4], replicated, may hold values from 2 to 6
- coefficients: int32 [4], replicated, may hold values from -3 to 3, as said below
- rates: float32 [2, 4], replicated, may hold values from 0.01 to 0.4, as said below
- reaction: float32 [1], replicated, may hold values from 0.1 to 0.3
Outputs:
- result: float32 [4, 256, 64, 256], P('comp', 'gx', 'gy')
Inputs may be any that keep to these rules, and one draw needn't show every extreme that they name: The fourth dimension of grid g has level 8 minus third_level[g]. `coefficients`: every weight is a nonzero integer; some are positive and some negative. `rates`: courant numbers of the first two dimensions lie from 0.3 to 0.4, all other entries from 0.01 to 0.02.
All inputs are finite; a program needn't handle non-finite values.
Results may differ from a plain program's by a relative error of at most 0.0003.
Values sent between devices are 32-bit elements; how exact they have to be, the bound alone decides.
No kernel may reach another device: no remote copies, remote signals or barrier semaphores. Data moves between devices by JAX's collectives and lax.ppermute only.
A program may use at most 128 MiB of HBM per device.

v0:
```python
import jax
import jax.numpy as jnp
import numpy as np
from jax import lax
from jax.sharding import PartitionSpec as P

SECTIONS = 4
LEVEL_SUM = 8


def extended(block, sides, width):
    for axis, dim in sides:
        count = lax.axis_size(axis)
        forward = [(i, i + 1) for i in range(count - 1)]
        forward.append((count - 1, 0))
        backward = [(target, source) for source, target in forward]
        low = lax.ppermute(
            lax.slice_in_dim(block, block.shape[dim] - width, None, axis=dim), axis, forward
        )
        high = lax.ppermute(lax.slice_in_dim(block, 0, width, axis=dim), axis, backward)
        block = jnp.concatenate([low, block, high], axis=dim)
    return block


def points(level):
    return 1 if level == 0 else 2 ** (level - 1)


def slot_table():
    top = LEVEL_SUM - 2
    table = np.zeros((top + 1) * (top + 1), np.int32)
    total = 0
    for first in range(top + 1):
        for second in range(top + 1):
            if first + second <= LEVEL_SUM:
                table[first * (top + 1) + second] = total
                total += points(first) * points(second)
    return (table, total)


def hier_level(index, level):
    zeros = jnp.zeros_like(index)
    for power in range(1, LEVEL_SUM + 1):
        zeros = zeros + (jnp.remainder(index, 2**power) == 0).astype(jnp.int32)
    depth = jnp.where(index == 0, 0, level - zeros)
    placed = jnp.where(index == 0, 0, jnp.right_shift(index, zeros + 1))
    return (depth, placed)


def fast_layout(level_a, size):
    level_b = LEVEL_SUM - level_a
    width = jnp.left_shift(jnp.int32(1), level_b)
    index = jnp.arange(size, dtype=jnp.int32)
    third = index // width
    return (width, third, index - third * width)


def slot_positions(level_a, table):
    top = LEVEL_SUM - 2
    size = 2**LEVEL_SUM
    width, third, fourth = fast_layout(level_a, size)
    depth_third, rank_third = hier_level(third, level_a)
    depth_fourth, rank_fourth = hier_level(fourth, LEVEL_SUM - level_a)
    count_fourth = jnp.where(
        depth_fourth == 0, 1, jnp.left_shift(jnp.int32(1), jnp.maximum(depth_fourth - 1, 0))
    )
    code = depth_third * (top + 1) + depth_fourth
    choose = code[:, None] == jnp.arange((top + 1) * (top + 1), dtype=jnp.int32)[None, :]
    offset = jnp.sum(jnp.where(choose, jnp.asarray(table)[None, :], 0), axis=1).astype(jnp.int32)
    return offset + rank_third * count_fourth + rank_fourth


def block_neighbours(values, shift, width, inner):
    ahead = jnp.where(
        inner + shift < width,
        jnp.roll(values, -shift, axis=-1),
        jnp.roll(values, width - shift, axis=-1),
    )
    behind = jnp.where(
        inner - shift >= 0,
        jnp.roll(values, shift, axis=-1),
        jnp.roll(values, shift - width, axis=-1),
    )
    return (ahead, behind)


def transform(values, level_a, forward):
    top = LEVEL_SUM - 2
    level_b = LEVEL_SUM - level_a
    width, third, fourth = fast_layout(level_a, values.shape[-1])
    depth_third = hier_level(third, level_a)[0]
    depth_fourth = hier_level(fourth, level_b)[0]
    factor = -0.5 if forward else 0.5

    def fourth_pass(values, level):
        shift = jnp.left_shift(jnp.int32(1), jnp.maximum(level_b - level, 0))
        ahead, behind = block_neighbours(values, shift, width, fourth)
        return jnp.where(depth_fourth == level, values + factor * (ahead + behind), values)

    def third_pass(values, level):
        shift = jnp.left_shift(jnp.int32(1), jnp.maximum(level_a - level, 0))
        ahead = jnp.roll(values, -shift * width, axis=-1)
        behind = jnp.roll(values, shift * width, axis=-1)
        return jnp.where(depth_third == level, values + factor * (ahead + behind), values)

    if forward:
        for level in range(top, 0, -1):
            values = fourth_pass(values, level)
        for level in range(top, 0, -1):
            values = third_pass(values, level)
    else:
        for level in range(1, top + 1):
            values = third_pass(values, level)
        for level in range(1, top + 1):
            values = fourth_pass(values, level)
    return values


def grid_rates(rates, level_a):
    top = LEVEL_SUM - 2
    level_b = LEVEL_SUM - level_a
    coarse_third = 1.0 / jnp.left_shift(jnp.int32(1), top - level_a).astype(jnp.float32)
    coarse_fourth = 1.0 / jnp.left_shift(jnp.int32(1), top - level_b).astype(jnp.float32)
    unity = jnp.ones((), jnp.float32)
    diffusion = rates[0] * jnp.stack(
        [unity, unity, coarse_third * coarse_third, coarse_fourth * coarse_fourth]
    )
    courant = rates[1] * jnp.stack([unity, unity, coarse_third, coarse_fourth])
    return (diffusion, courant)


def advance(padded, diffusion, courant, rate, width, fourth):
    centre = padded[1:-1, 1:-1]
    up_first = padded[2:, 1:-1]
    down_first = padded[:-2, 1:-1]
    up_second = padded[1:-1, 2:]
    down_second = padded[1:-1, :-2]
    up_third = jnp.roll(centre, -width, axis=-1)
    down_third = jnp.roll(centre, width, axis=-1)
    up_fourth, down_fourth = block_neighbours(centre, 1, width, fourth)
    change = diffusion[0] * (up_first - 2.0 * centre + down_first) - courant[0] * (
        centre - down_first
    )
    change = (
        change
        + diffusion[1] * (up_second - 2.0 * centre + down_second)
        - courant[1] * (centre - down_second)
    )
    change = (
        change
        + diffusion[2] * (up_third - 2.0 * centre + down_third)
        - courant[2] * (centre - down_third)
    )
    change = (
        change
        + diffusion[3] * (up_fourth - 2.0 * centre + down_fourth)
        - courant[3] * (centre - down_fourth)
    )
    return centre + change + rate * centre / (1.0 + centre * centre)


def local(field, third_level, coefficients, rates, reaction):
    grid = lax.axis_index("comp")
    level_a = lax.dynamic_index_in_dim(third_level, grid, 0, False)
    weight = lax.dynamic_index_in_dim(coefficients, grid, 0, False).astype(jnp.float32)
    diffusion, courant = grid_rates(rates, level_a)
    size = field.shape[-1]
    width, third, fourth = fast_layout(level_a, size)
    values = field[0]
    for section in range(SECTIONS):
        padded = extended(values, (("gx", 0), ("gy", 1)), 1)
        values = advance(padded, diffusion, courant, reaction[0], width, fourth)
    surplus = transform(values, level_a, True) * weight
    table, total_slots = slot_table()
    own_slots = slot_positions(level_a, table)
    columns = jnp.arange(size, dtype=jnp.int32)
    carry = jnp.zeros_like(surplus)
    piece = lax.all_gather(surplus[None], "comp", axis=0, tiled=True)

    def add_grid(inner, item):
        remote, source_grid = item
        other_level = lax.dynamic_index_in_dim(third_level, source_grid, 0, False)
        other_slots = slot_positions(other_level, table)
        match = other_slots[None, :] == own_slots[:, None]
        source = jnp.sum(jnp.where(match, columns[None, :], 0), axis=1)
        found = jnp.any(match, axis=1)
        return (inner + jnp.where(found, jnp.take(remote, source, axis=-1), 0.0), None)

    sources = jnp.arange(piece.shape[0], dtype=jnp.int32)
    carry, unused = lax.scan(add_grid, carry, (piece, sources))
    return transform(carry, level_a, False)[None]


def solution(mesh):
    return jax.shard_map(
        local,
        mesh=mesh,
        in_specs=(P("comp", "gx", "gy", None), P(), P(), P(), P()),
        out_specs=P("comp", "gx", "gy", None),
        check_vma=False,
    )
```

profile of v0, /device:TPU:0, one launch (start us, length us, event | category | flops | bytes accessed | tf_op | source)
XLA Modules:
  0.0 363.2 jit_solution(3005916287803881157)
XLA Ops:
  31.7 4.1 %collective-permute-start.2 = (f32[130,1,256]{2,1,0:T(1,128)S(1)}, f32[130,1,256]{2,1,0:T(1,128)S(1)}, u32[]{:S(2)}, u32[]{:S(2)}) collective-permute-start(f32[130,1,256]{2,1,0:T(1,128)S(1)} %get-tuple-element.253), channel_id=1, source_target_pairs={{1,0},{2,1},{3,2},{0,3},{5,4},{6,5},{7,6},{4,7},{9,8},{10,9},{11,1... | collective-permute-start | bytes 399368 | tf_op jit(solution)/shard_map/ppermute | solution.py:20
  42.7 15.4 %fusion.254 = f32[128,16,256]{2,1,0:T(8,128)S(1)} fusion(f32[128,16,256]{2,1,0:T(8,128)S(1)} %bitcast.54, s32[]{:T(128)S(6)} %select_n.1227, s32[]{:T(128)S(6)} %select_n.1231, f32[1,16,256]{2,1,0:T(8,128)} %copy-done.2, f32[130,1,256]{2,1,0:T(1,128)} %collective-permute-done.3, f32[1,16,256]{2,1,0:T(8,128)} %copy-done.1, ...), kind=kLoop, calls=%fused_computation.525 | loop fusion | flops 26214400 | bytes 8688180 | tf_op jit(solution)/shard_map/add | solution.py:159
  69.7 4.7 %collective-permute-done.7 = f32[130,1,256]{2,1,0:T(1,128)S(1)} collective-permute-done((f32[130,1,256]{2,1,0:T(1,128)S(1)}, f32[130,1,256]{2,1,0:T(1,128)S(1)}, u32[]{:S(2)}, u32[]{:S(2)}) %collective-permute-start.7) | collective-permute-done | bytes 133152 | tf_op jit(solution)/shard_map/ppermute | solution.py:17
  74.4 14.6 %fusion.229 = f32[128,16,256]{2,1,0:T(8,128)S(1)} fusion(f32[128,16,256]{2,1,0:T(8,128)S(1)} %fusion.254, s32[]{:T(128)S(6)} %select_n.1227, s32[]{:T(128)S(6)} %select_n.1231, f32[1,16,256]{2,1,0:T(8,128)S(1)} %collective-permute-done.4, f32[130,1,256]{2,1,0:T(1,128)S(1)} %collective-permute-done.7, f32[1,16,256]{2,1,0:T(8,128)S(1)} %collective-permute-done.5, ...), kind=kLoop, calls=%fused_computation.498 | loop fusion | flops 26214400 | bytes 8688180 | tf_op jit(solution)/shard_map/add | solution.py:159
  100.4 14.5 %fusion.204 = f32[128,16,256]{2,1,0:T(8,128)S(1)} fusion(f32[128,16,256]{2,1,0:T(8,128)S(1)} %fusion.229, s32[]{:T(128)S(6)} %select_n.1227, s32[]{:T(128)S(6)} %select_n.1231, f32[1,16,256]{2,1,0:T(8,128)S(1)} %collective-permute-done.8, f32[130,1,256]{2,1,0:T(1,128)S(1)} %collective-permute-done.11, f32[1,16,256]{2,1,0:T(8,128)S(1)} %collective-permute-done.9, ...), kind=kLoop, calls=%fused_computation.471 | loop fusion | flops 26214400 | bytes 8688180 | tf_op jit(solution)/shard_map/add | solution.py:159
  127.4 14.7 %fusion.179 = f32[128,16,256]{2,1,0:T(8,128)S(1)} fusion(f32[128,16,256]{2,1,0:T(8,128)S(1)} %fusion.204, s32[]{:T(128)S(6)} %select_n.1227, s32[]{:T(128)S(6)} %select_n.1231, f32[1,16,256]{2,1,0:T(8,128)S(1)} %collective-permute-done.12, f32[130,1,256]{2,1,0:T(1,128)S(1)} %collective-permute-done.15, f32[1,16,256]{2,1,0:T(8,128)S(1)} %collective-permute-done.13, ...), kind=kLoop, calls=%fused_computation.444 | loop fusion | flops 26214400 | bytes 8688180 | tf_op jit(solution)/shard_map/add | solution.py:159
  142.2 4.6 %add_select_fusion.23 = f32[128,16,256]{2,1,0:T(8,128)S(1)} fusion(f32[128,16,256]{2,1,0:T(8,128)S(1)} %fusion.179, s32[]{:T(128)S(6)} %select_n.1265, s32[]{:T(128)S(6)} %select_n.1259, s32[]{:T(128)S(6)} %select_n.1261, s32[]{:T(128)S(6)} %select_n.1263, pred[256]{0:T(512)(128)(4,1)S(1)} %copy-done.9, pred[256]{0:T(512)(128)(4,1)S(1)} %copy-done.10, ...), kind=kLoop, calls=%fused_computation.286 | loop fusion | flops 5242880 | bytes 4195088 | tf_op jit(solution)/shard_map/jit(_where)/select_n | solution.py:98
  146.8 4.5 %add_select_fusion.22 = f32[128,16,256]{2,1,0:T(8,128)S(1)} fusion(f32[128,16,256]{2,1,0:T(8,128)S(1)} %add_select_fusion.23, s32[]{:T(128)S(6)} %select_n.1273, s32[]{:T(128)S(6)} %select_n.1267, s32[]{:T(128)S(6)} %select_n.1269, s32[]{:T(128)S(6)} %select_n.1271, pred[256]{0:T(512)(128)(4,1)S(1)} %copy-done.19, pred[256]{0:T(512)(128)(4,1)S(1)} %copy-done.20, ...), kind=kLoop, calls=%fused_computation.285 | loop fusion | flops 5242880 | bytes 4195088 | tf_op jit(solution)/shard_map/jit(_where)/select_n | solution.py:98
  151.5 4.8 %add_select_fusion.21 = f32[128,16,256]{2,1,0:T(8,128)S(1)} fusion(f32[128,16,256]{2,1,0:T(8,128)S(1)} %add_select_fusion.22, s32[]{:T(128)S(6)} %select_n.1281, s32[]{:T(128)S(6)} %select_n.1275, s32[]{:T(128)S(6)} %select_n.1277, s32[]{:T(128)S(6)} %select_n.1279, pred[256]{0:T(512)(128)(4,1)S(1)} %copy-done.12, pred[256]{0:T(512)(128)(4,1)S(1)} %copy-done.13, ...), kind=kLoop, calls=%fused_computation.284 | loop fusion | flops 5242880 | bytes 4195088 | tf_op jit(solution)/shard_map/jit(_where)/select_n | solution.py:98
  156.4 4.6 %add_select_fusion.20 = f32[128,16,256]{2,1,0:T(8,128)S(1)} fusion(f32[128,16,256]{2,1,0:T(8,128)S(1)} %add_select_fusion.21, s32[]{:T(128)S(6)} %select_n.1289, s32[]{:T(128)S(6)} %select_n.1283, s32[]{:T(128)S(6)} %select_n.1285, s32[]{:T(128)S(6)} %select_n.1287, pred[256]{0:T(512)(128)(4,1)S(1)} %copy-done.15, pred[256]{0:T(512)(128)(4,1)S(1)} %copy-done.16, ...), kind=kLoop, calls=%fused_computation.283 | loop fusion | flops 5242880 | bytes 4195088 | tf_op jit(solution)/shard_map/jit(_where)/select_n | solution.py:98
  161.0 4.5 %add_select_fusion.19 = f32[128,16,256]{2,1,0:T(8,128)S(1)} fusion(f32[128,16,256]{2,1,0:T(8,128)S(1)} %add_select_fusion.20, s32[]{:T(128)S(6)} %select_n.1297, s32[]{:T(128)S(6)} %select_n.1291, s32[]{:T(128)S(6)} %select_n.1293, s32[]{:T(128)S(6)} %select_n.1295, pred[256]{0:T(512)(128)(4,1)S(1)} %copy-done.21, pred[256]{0:T(512)(128)(4,1)S(1)} %copy-done.22, ...), kind=kLoop, calls=%fused_computation.282 | loop fusion | flops 5242880 | bytes 4195088 | tf_op jit(solution)/shard_map/jit(_where)/select_n | solution.py:98
  165.6 5.0 %add_select_fusion.18 = f32[128,16,256]{2,1,0:T(8,128)S(1)} fusion(f32[128,16,256]{2,1,0:T(8,128)S(1)} %add_select_fusion.19, s32[]{:T(128)S(6)} %select_n.1305, s32[]{:T(128)S(6)} %select_n.1299, s32[]{:T(128)S(6)} %select_n.1301, s32[]{:T(128)S(6)} %select_n.1303, pred[256]{0:T(512)(128)(4,1)S(1)} %copy-done.24, pred[256]{0:T(512)(128)(4,1)S(1)} %copy-done.25, ...), kind=kLoop, calls=%fused_computation.281 | loop fusion | flops 5242880 | bytes 4195088 | tf_op jit(solution)/shard_map/jit(_where)/select_n | solution.py:98
  186.9 55.7 %all-gather.3.cloned.1.call-done = f32[512,16,256]{2,1,0:T(8,128)} async-done(((f32[128,16,256]{2,1,0:T(8,128)}), f32[512,16,256]{2,1,0:T(8,128)}) %all-gather.3.cloned.1.call-update) | async-done | bytes 8388624 | tf_op jit(solution)/shard_map/all_gather | solution.py:178
  242.6 63.3 %while.15 = (s32[]{:T(128)}, f32[128,16,256]{0,1,2:T(8,128)}, s32[4]{0:T(128)S(1)}, s32[4]{0:T(128)S(1)}, s32[256]{0:T(256)S(1)}, /*index=5*/f32[4,128,16,256]{3...) while((s32[]{:T(128)}, f32[128,16,256]{0,1,2:T(8,128)}, ...), condition=%wide.region_5.7_spmd.clone.clone, body=%wide.region_1.6_spmd.sunk.clone.clone.sunk | while | flops 2568969 | bytes 18895292 | solution.py:190
  269.2 4.2 %bitcast_add_fusion.2 = f32[128,16,256]{0,1,2:T(8,128)} fusion(f32[128,16,256]{0,1,2:T(8,128)} %get-tuple-element.368, f32[256,128,16]{1,2,0:T(8,128)S(1)} %gather_fusion, pred[256]{0:T(512)(128)(4,1)S(1)} %compare_reduce_fusion.2, pred[256]{0:T(512)(128)(4,1)S(1)} %compare_and_fusion.2, pred[]{:T(512)S(6)} %compare.116), kind=kLoop, calls=%fused_computation.2.clone.1 | loop fusion | flops 2097152 | bytes 6291969 | tf_op jit(solution)/shard_map/while/body/eval_jaxpr/add | solution.py:187
  285.4 4.2 %bitcast_add_fusion.2 = f32[128,16,256]{0,1,2:T(8,128)} fusion(f32[128,16,256]{0,1,2:T(8,128)} %get-tuple-element.368, f32[256,128,16]{1,2,0:T(8,128)S(1)} %gather_fusion, pred[256]{0:T(512)(128)(4,1)S(1)} %compare_reduce_fusion.2, pred[256]{0:T(512)(128)(4,1)S(1)} %compare_and_fusion.2, pred[]{:T(512)S(6)} %compare.116), kind=kLoop, calls=%fused_computation.2.clone.1 | loop fusion | flops 2097152 | bytes 6291969 | tf_op jit(solution)/shard_map/while/body/eval_jaxpr/add | solution.py:187
  301.6 4.2 %bitcast_add_fusion.2 = f32[128,16,256]{0,1,2:T(8,128)} fusion(f32[128,16,256]{0,1,2:T(8,128)} %get-tuple-element.368, f32[256,128,16]{1,2,0:T(8,128)S(1)} %gather_fusion, pred[256]{0:T(512)(128)(4,1)S(1)} %compare_reduce_fusion.2, pred[256]{0:T(512)(128)(4,1)S(1)} %compare_and_fusion.2, pred[]{:T(512)S(6)} %compare.116), kind=kLoop, calls=%fused_computation.2.clone.1 | loop fusion | flops 2097152 | bytes 6291969 | tf_op jit(solution)/shard_map/while/body/eval_jaxpr/add | solution.py:187
  309.2 6.1 %add_select_fusion.11 = f32[128,16,256]{2,1,0:T(8,128)S(1)} fusion(f32[128,16,256]{2,1,0:T(8,128)} %copy.26, s32[]{:T(128)S(6)} %select_n.1329, s32[]{:T(128)S(6)} %select_n.1327, pred[256]{0:T(512)(128)(4,1)S(1)} %copy-done.31), kind=kLoop, calls=%fused_computation.274 | loop fusion | flops 3145728 | bytes 4194568 | tf_op jit(solution)/shard_map/jit(_where)/select_n | solution.py:104
  327.0 4.6 %add_select_fusion.5 = f32[128,16,256]{2,1,0:T(8,128)S(1)} fusion(f32[128,16,256]{2,1,0:T(8,128)S(1)} %add_select_fusion.6, s32[]{:T(128)S(6)} %select_n.1305, s32[]{:T(128)S(6)} %select_n.1299, s32[]{:T(128)S(6)} %select_n.1301, s32[]{:T(128)S(6)} %select_n.1303, pred[256]{0:T(512)(128)(4,1)S(1)} %copy-done.24, pred[256]{0:T(512)(128)(4,1)S(1)} %copy-done.25, ...), kind=kLoop, calls=%fused_computation.268 | loop fusion | flops 5242880 | bytes 4195088 | tf_op jit(solution)/shard_map/jit(_where)/select_n | solution.py:98
  331.6 4.5 %add_select_fusion.4 = f32[128,16,256]{2,1,0:T(8,128)S(1)} fusion(f32[128,16,256]{2,1,0:T(8,128)S(1)} %add_select_fusion.5, s32[]{:T(128)S(6)} %select_n.1297, s32[]{:T(128)S(6)} %select_n.1291, s32[]{:T(128)S(6)} %select_n.1293, s32[]{:T(128)S(6)} %select_n.1295, pred[256]{0:T(512)(128)(4,1)S(1)} %copy-done.21, pred[256]{0:T(512)(128)(4,1)S(1)} %copy-done.22, ...), kind=kLoop, calls=%fused_computation.267 | loop fusion | flops 5242880 | bytes 4195088 | tf_op jit(solution)/shard_map/jit(_where)/select_n | solution.py:98
  336.2 4.8 %add_select_fusion.3 = f32[128,16,256]{2,1,0:T(8,128)S(1)} fusion(f32[128,16,256]{2,1,0:T(8,128)S(1)} %add_select_fusion.4, s32[]{:T(128)S(6)} %select_n.1289, s32[]{:T(128)S(6)} %select_n.1283, s32[]{:T(128)S(6)} %select_n.1285, s32[]{:T(128)S(6)} %select_n.1287, pred[256]{0:T(512)(128)(4,1)S(1)} %copy-done.15, pred[256]{0:T(512)(128)(4,1)S(1)} %copy-done.16, ...), kind=kLoop, calls=%fused_computation.266 | loop fusion | flops 5242880 | bytes 4195088 | tf_op jit(solution)/shard_map/jit(_where)/select_n | solution.py:98
  341.0 4.5 %add_select_fusion.2 = f32[128,16,256]{2,1,0:T(8,128)S(1)} fusion(f32[128,16,256]{2,1,0:T(8,128)S(1)} %add_select_fusion.3, s32[]{:T(128)S(6)} %select_n.1281, s32[]{:T(128)S(6)} %select_n.1275, s32[]{:T(128)S(6)} %select_n.1277, s32[]{:T(128)S(6)} %select_n.1279, pred[256]{0:T(512)(128)(4,1)S(1)} %copy-done.12, pred[256]{0:T(512)(128)(4,1)S(1)} %copy-done.13, ...), kind=kLoop, calls=%fused_computation.265 | loop fusion | flops 5242880 | bytes 4195088 | tf_op jit(solution)/shard_map/jit(_where)/select_n | solution.py:98
  345.5 4.8 %add_select_fusion.1 = f32[128,16,256]{2,1,0:T(8,128)S(1)} fusion(f32[128,16,256]{2,1,0:T(8,128)S(1)} %add_select_fusion.2, s32[]{:T(128)S(6)} %select_n.1273, s32[]{:T(128)S(6)} %select_n.1267, s32[]{:T(128)S(6)} %select_n.1269, s32[]{:T(128)S(6)} %select_n.1271, pred[256]{0:T(512)(128)(4,1)S(1)} %copy-done.19, pred[256]{0:T(512)(128)(4,1)S(1)} %copy-done.20, ...), kind=kLoop, calls=%fused_computation.264 | loop fusion | flops 5242880 | bytes 4195088 | tf_op jit(solution)/shard_map/jit(_where)/select_n | solution.py:98
  350.3 5.8 %fusion.23 = f32[1,128,16,256]{3,2,1,0:T(8,128)} fusion(f32[128,16,256]{2,1,0:T(8,128)S(1)} %add_select_fusion.1, s32[]{:T(128)S(6)} %select_n.1265, s32[]{:T(128)S(6)} %select_n.1259, s32[]{:T(128)S(6)} %select_n.1261, s32[]{:T(128)S(6)} %select_n.1263, pred[256]{0:T(512)(128)(4,1)S(1)} %copy-done.9, pred[256]{0:T(512)(128)(4,1)S(1)} %copy-done.10, ...), kind=kLoop, calls=%fused_computation.288 | loop fusion | flops 5242880 | bytes 4195088 | tf_op jit(solution)/shard_map/broadcast_in_dim | solution.py:191
  (201 shorter events, 128.4 us)
Async XLA Ops:
  6.5 236.0 %all-gather.3.cloned.1.call-start = ((), (), s32[]{:S(2)}) async-start(), calls=%async_computation | async-start | bytes 10485760 | tf_op jit(solution)/shard_map/all_gather | solution.py:178
  7.3 23.8 %collective-permute-start.1 = (f32[1,16,256]{2,1,0:T(8,128)S(1)}, f32[1,16,256]{2,1,0:T(8,128)S(1)}, u32[]{:S(2)}, u32[]{:S(2)}) collective-permute-start(f32[1,16,256]{2,1,0:T(8,128)S(1)} %get-tuple-element.277), channel_id=1, source_target_pairs={{0,4},{4,0},{1,5},{5,1},{2,6},{6,2},{3,7},{7,3},{8,12},{12,8},{9,1... | collective-permute-start | bytes 49160 | tf_op jit(solution)/shard_map/ppermute | solution.py:17
  10.2 20.8 %collective-permute-start = (f32[1,16,256]{2,1,0:T(8,128)S(1)}, f32[1,16,256]{2,1,0:T(8,128)S(1)}, u32[]{:S(2)}, u32[]{:S(2)}) collective-permute-start(f32[1,16,256]{2,1,0:T(8,128)S(1)} %get-tuple-element.278), channel_id=1, source_target_pairs={{4,0},{0,4},{5,1},{1,5},{6,2},{2,6},{7,3},{3,7},{12,8},{8,12},{13,... | collective-permute-start | bytes 49160 | tf_op jit(solution)/shard_map/ppermute | solution.py:20
  15.1 12.2 %copy-start.6 = (s32[256]{0:T(256)}, s32[256]{0:T(256)S(1)}, u32[]{:S(2)}) copy-start(s32[256]{0:T(256)S(1)} %get-tuple-element.244) | copy-start | bytes 3076
  18.1 9.8 %copy-start.32 = (f32[2,4]{1,0:T(2,128)S(1)}, f32[2,4]{1,0:T(2,128)}, u32[]{:S(2)}) copy-start(f32[2,4]{1,0:T(2,128)} %param.13) | copy-start | bytes 100
  31.7 10.7 %collective-permute-start.2 = (f32[130,1,256]{2,1,0:T(1,128)S(1)}, f32[130,1,256]{2,1,0:T(1,128)S(1)}, u32[]{:S(2)}, u32[]{:S(2)}) collective-permute-start(f32[130,1,256]{2,1,0:T(1,128)S(1)} %get-tuple-element.253), channel_id=1, source_target_pairs={{1,0},{2,1},{3,2},{0,3},{5,4},{6,5},{7,6},{4,7},{9,8},{10,9},{11,1... | collective-permute-start | bytes 399368 | tf_op jit(solution)/shard_map/ppermute | solution.py:20
  35.8 6.9 %collective-permute-start.3 = (f32[130,1,256]{2,1,0:T(1,128)S(1)}, f32[130,1,256]{2,1,0:T(1,128)}, u32[]{:S(2)}, u32[]{:S(2)}) collective-permute-start(f32[130,1,256]{2,1,0:T(1,128)S(1)} %get-tuple-element.254), channel_id=1, source_target_pairs={{0,1},{1,2},{2,3},{3,0},{4,5},{5,6},{6,7},{7,4},{8,9},{9,10},{10,1... | collective-permute-start | bytes 399368 | tf_op jit(solution)/shard_map/ppermute | solution.py:17
  58.1 3.8 %collective-permute-start.5 = (f32[1,16,256]{2,1,0:T(8,128)S(1)}, f32[1,16,256]{2,1,0:T(8,128)S(1)}, u32[]{:S(2)}, u32[]{:S(2)}) collective-permute-start(f32[1,16,256]{2,1,0:T(8,128)S(1)} %get-tuple-element.271), channel_id=1, source_target_pairs={{0,4},{4,0},{1,5},{5,1},{2,6},{6,2},{3,7},{7,3},{8,12},{12,8},{9,1... | collective-permute-start | bytes 49160 | tf_op jit(solution)/shard_map/ppermute | solution.py:17
  59.6 3.7 %collective-permute-start.4 = (f32[1,16,256]{2,1,0:T(8,128)S(1)}, f32[1,16,256]{2,1,0:T(8,128)S(1)}, u32[]{:S(2)}, u32[]{:S(2)}) collective-permute-start(f32[1,16,256]{2,1,0:T(8,128)S(1)} %get-tuple-element.272), channel_id=1, source_target_pairs={{4,0},{0,4},{5,1},{1,5},{6,2},{2,6},{7,3},{3,7},{12,8},{8,12},{13,... | collective-permute-start | bytes 49160 | tf_op jit(solution)/shard_map/ppermute | solution.py:20
  63.6 6.1 %collective-permute-start.6 = (f32[130,1,256]{2,1,0:T(1,128)S(1)}, f32[130,1,256]{2,1,0:T(1,128)S(1)}, u32[]{:S(2)}, u32[]{:S(2)}) collective-permute-start(f32[130,1,256]{2,1,0:T(1,128)S(1)} %get-tuple-element.251), channel_id=1, source_target_pairs={{1,0},{2,1},{3,2},{0,3},{5,4},{6,5},{7,6},{4,7},{9,8},{10,9},{11,1... | collective-permute-start | bytes 399368 | tf_op jit(solution)/shard_map/ppermute | solution.py:20
  67.2 7.2 %copy-start.5 = (pred[256]{0:T(512)(128)(4,1)S(1)}, pred[256]{0:T(512)(128)(4,1)}, u32[]{:S(2)}) copy-start(pred[256]{0:T(512)(128)(4,1)} %get-tuple-element.312) | copy-start | bytes 772
  67.2 7.2 %collective-permute-start.7 = (f32[130,1,256]{2,1,0:T(1,128)S(1)}, f32[130,1,256]{2,1,0:T(1,128)S(1)}, u32[]{:S(2)}, u32[]{:S(2)}) collective-permute-start(f32[130,1,256]{2,1,0:T(1,128)S(1)} %get-tuple-element.252), channel_id=1, source_target_pairs={{0,1},{1,2},{2,3},{3,0},{4,5},{5,6},{6,7},{7,4},{8,9},{9,10},{10,1... | collective-permute-start | bytes 399368 | tf_op jit(solution)/shard_map/ppermute | solution.py:17
  89.0 3.8 %collective-permute-start.9 = (f32[1,16,256]{2,1,0:T(8,128)S(1)}, f32[1,16,256]{2,1,0:T(8,128)S(1)}, u32[]{:S(2)}, u32[]{:S(2)}) collective-permute-start(f32[1,16,256]{2,1,0:T(8,128)S(1)} %get-tuple-element.265), channel_id=1, source_target_pairs={{0,4},{4,0},{1,5},{5,1},{2,6},{6,2},{3,7},{7,3},{8,12},{12,8},{9,1... | collective-permute-start | bytes 49160 | tf_op jit(solution)/shard_map/ppermute | solution.py:17
  89.6 3.7 %collective-permute-start.8 = (f32[1,16,256]{2,1,0:T(8,128)S(1)}, f32[1,16,256]{2,1,0:T(8,128)S(1)}, u32[]{:S(2)}, u32[]{:S(2)}) collective-permute-start(f32[1,16,256]{2,1,0:T(8,128)S(1)} %get-tuple-element.266), channel_id=1, source_target_pairs={{4,0},{0,4},{5,1},{1,5},{6,2},{2,6},{7,3},{3,7},{12,8},{8,12},{13,... | collective-permute-start | bytes 49160 | tf_op jit(solution)/shard_map/ppermute | solution.py:20
  93.5 5.0 %collective-permute-start.10 = (f32[130,1,256]{2,1,0:T(1,128)S(1)}, f32[130,1,256]{2,1,0:T(1,128)S(1)}, u32[]{:S(2)}, u32[]{:S(2)}) collective-permute-start(f32[130,1,256]{2,1,0:T(1,128)S(1)} %get-tuple-element.249), channel_id=1, source_target_pairs={{1,0},{2,1},{3,2},{0,3},{5,4},{6,5},{7,6},{4,7},{9,8},{10,9},{11,1... | collective-permute-start | bytes 399368 | tf_op jit(solution)/shard_map/ppermute | solution.py:20
  93.6 6.8 %collective-permute-start.11 = (f32[130,1,256]{2,1,0:T(1,128)S(1)}, f32[130,1,256]{2,1,0:T(1,128)S(1)}, u32[]{:S(2)}, u32[]{:S(2)}) collective-permute-start(f32[130,1,256]{2,1,0:T(1,128)S(1)} %get-tuple-element.250), channel_id=1, source_target_pairs={{0,1},{1,2},{2,3},{3,0},{4,5},{5,6},{6,7},{7,4},{8,9},{9,10},{10,1... | collective-permute-start | bytes 399368 | tf_op jit(solution)/shard_map/ppermute | solution.py:17
  115.0 3.8 %collective-permute-start.13 = (f32[1,16,256]{2,1,0:T(8,128)S(1)}, f32[1,16,256]{2,1,0:T(8,128)S(1)}, u32[]{:S(2)}, u32[]{:S(2)}) collective-permute-start(f32[1,16,256]{2,1,0:T(8,128)S(1)} %get-tuple-element.259), channel_id=1, source_target_pairs={{0,4},{4,0},{1,5},{5,1},{2,6},{6,2},{3,7},{7,3},{8,12},{12,8},{9,1... | collective-permute-start | bytes 49160 | tf_op jit(solution)/shard_map/ppermute | solution.py:17
  116.5 3.7 %collective-permute-start.12 = (f32[1,16,256]{2,1,0:T(8,128)S(1)}, f32[1,16,256]{2,1,0:T(8,128)S(1)}, u32[]{:S(2)}, u32[]{:S(2)}) collective-permute-start(f32[1,16,256]{2,1,0:T(8,128)S(1)} %get-tuple-element.260), channel_id=1, source_target_pairs={{4,0},{0,4},{5,1},{1,5},{6,2},{2,6},{7,3},{3,7},{12,8},{8,12},{13,... | collective-permute-start | bytes 49160 | tf_op jit(solution)/shard_map/ppermute | solution.py:20
  120.5 5.0 %collective-permute-start.14 = (f32[130,1,256]{2,1,0:T(1,128)S(1)}, f32[130,1,256]{2,1,0:T(1,128)S(1)}, u32[]{:S(2)}, u32[]{:S(2)}) collective-permute-start(f32[130,1,256]{2,1,0:T(1,128)S(1)} %get-tuple-element.247), channel_id=1, source_target_pairs={{1,0},{2,1},{3,2},{0,3},{5,4},{6,5},{7,6},{4,7},{9,8},{10,9},{11,1... | collective-permute-start | bytes 399368 | tf_op jit(solution)/shard_map/ppermute | solution.py:20
  120.6 6.8 %collective-permute-start.15 = (f32[130,1,256]{2,1,0:T(1,128)S(1)}, f32[130,1,256]{2,1,0:T(1,128)S(1)}, u32[]{:S(2)}, u32[]{:S(2)}) collective-permute-start(f32[130,1,256]{2,1,0:T(1,128)S(1)} %get-tuple-element.248), channel_id=1, source_target_pairs={{0,1},{1,2},{2,3},{3,0},{4,5},{5,6},{6,7},{7,4},{8,9},{9,10},{10,1... | collective-permute-start | bytes 399368 | tf_op jit(solution)/shard_map/ppermute | solution.py:17
  127.4 14.7 %copy-start.9 = (pred[256]{0:T(512)(128)(4,1)S(1)}, pred[256]{0:T(512)(128)(4,1)}, u32[]{:S(2)}) copy-start(pred[256]{0:T(512)(128)(4,1)} %get-tuple-element.309) | copy-start | bytes 772
  127.4 14.7 %copy-start.10 = (pred[256]{0:T(512)(128)(4,1)S(1)}, pred[256]{0:T(512)(128)(4,1)}, u32[]{:S(2)}) copy-start(pred[256]{0:T(512)(128)(4,1)} %get-tuple-element.310) | copy-start | bytes 772
  127.4 14.8 %copy-start.11 = (pred[256]{0:T(512)(128)(4,1)S(1)}, pred[256]{0:T(512)(128)(4,1)}, u32[]{:S(2)}) copy-start(pred[256]{0:T(512)(128)(4,1)} %get-tuple-element.290) | copy-start | bytes 772
  186.0 56.6 %copy-start.33 = (s32[4]{0:T(128)S(1)}, s32[4]{0:T(128)}, u32[]{:S(2)}) copy-start(s32[4]{0:T(128)} %param.11) | copy-start | bytes 52
  (27 other events, 99.4 us)
Sparse Core Ops, SparseCore 0:
  186.1 56.3 all-gather.2
where the time goes:
time: 370 us; the launch traced here: 363 us
  other arithmetic  180 us (49%)
  waiting for transfers between devices  77.8 us (21%)
  local copies, waits for them, and re-layouts  49 us (13%)
  between operations  23.9 us (6%)
  starting transfers between devices  21.6 us (6%)
  loops' own time  11.2 us (3%)
    add x4, other arithmetic, advance(): return centre + change + rate * centre / (1.0 + centre * centre)  59.2 us
    all_gather x1, waiting for transfers between devices, local(): piece = lax.all_gather(surplus[None], 'comp', axis=0, tiled=True)  55.7 us
    select_n x11, other arithmetic, fourth_pass(): jnp.where(depth_fourth == level, values + factor * (ahead + behind), values)  51.5 us
    select_n x11, other arithmetic, third_pass(): jnp.where(depth_third == level, values + factor * (ahead + behind), values)  29.3 us
    dynamic_slice x12, local copies, waits for them, and re-layouts, local(): carry, unused = lax.scan(add_grid, carry, (piece, sources))  18.7 us
    add x4, other arithmetic, add_grid(): inner + jnp.where(found, jnp.take(remote, source, axis=-1), 0.0)  15.3 us
    ppermute x8, waiting for transfers between devices, extended(): lax.ppermute(lax.slice_in_dim(block, block.shape[dim] - width, None, axis...  11.6 us
    another operation x1, loops' own time, local(): carry, unused = lax.scan(add_grid, carry, (piece, sources))  11.2 us
  transfers between devices with their start and end apart: 17, of which 14 were waited for; matrix products, arithmetic and copies ran while one was open for 6% of the time, Pallas kernels for 0%

commit v1 on v0

--- a/solution.py
+++ b/solution.py
@@ -175,7 +175,23 @@
     own_slots = slot_positions(level_a, table)
     columns = jnp.arange(size, dtype=jnp.int32)
     carry = jnp.zeros_like(surplus)
-    piece = lax.all_gather(surplus[None], "comp", axis=0, tiled=True)
+    ways, here, hop = (lax.axis_size("comp"), lax.axis_index("comp"), surplus[None].shape[0])
+    shape = [n * ways if d == 0 else n for d, n in enumerate(surplus[None].shape)]
+    full = lax.dynamic_update_slice_in_dim(
+        jnp.zeros(shape, surplus[None].dtype), surplus[None], here * hop, axis=0
+    )
+    going_up = going_down = surplus[None]
+    for far in range(1, ways // 2 + 1):
+        going_up = lax.ppermute(going_up, "comp", [(d, (d + 1) % ways) for d in range(ways)])
+        full = lax.dynamic_update_slice_in_dim(full, going_up, (here - far) % ways * hop, axis=0)
+        if 2 * far < ways:
+            going_down = lax.ppermute(
+                going_down, "comp", [(d, (d - 1) % ways) for d in range(ways)]
+            )
+            full = lax.dynamic_update_slice_in_dim(
+                full, going_down, (here + far) % ways * hop, axis=0
+            )
+    piece = full
 
     def add_grid(inner, item):
         remote, source_grid = item

time: 370 us -> 365 us (0.986)
  local copies, waits for them, and re-layouts: 49 us -> 65.3 us
  between operations: 23.9 us -> 11.2 us
  other arithmetic: 180 us -> 175 us
  waiting for transfers between devices: 77.8 us -> 73.3 us
    all_gather x1 -> x0, waiting for transfers between devices: 55.7 us -> none  [local(): piece = lax.all_gather(surplus[None], 'comp', axis=0, tiled=True)]
    ppermute x0 -> x3, waiting for transfers between devices: none -> 51.5 us  [the longest x2 51.5 us: local(): lax.ppermute(going_up, 'comp', [(d, (d + 1) % ways) for d in range(ways)])]
    dynamic_slice x12 -> x4, local copies, waits for them, and re-layouts: 18.7 us -> 2.3 us  [local(): carry, unused = lax.scan(add_grid, carry, (piece, sources))]
    squeeze x0 -> x4, local copies, waits for them, and re-layouts: none -> 12.1 us  [local(): carry, unused = lax.scan(add_grid, carry, (piece, sources))]
    ppermute x0 -> x3, local copies, waits for them, and re-layouts: none -> 9.33 us  [the longest x2 5.85 us: local(): lax.ppermute(going_up, 'comp', [(d, (d + 1) % ways) for d in range(ways)])]
    broadcast_in_dim x0 -> x2, local copies, waits for them, and re-layouts: none -> 6.32 us  [the longest x1 4.05 us: local(): jnp.zeros(shape, surplus[None].dtype)]
    dynamic_update_slice x0 -> x4, local copies, waits for them, and re-layouts: none -> 5.94 us  [the longest x2 3.01 us: local(): lax.dynamic_update_slice_in_dim(full, going_up, (here - far) % ways * hop...]
    ppermute x8, starting transfers between devices: 10.5 us -> 14.8 us  [extended(): lax.ppermute(lax.slice_in_dim(block, 0, width, axis=dim), axis, backward)]
  transfers between devices with their start and end apart: 17 -> 19, of which waited for: 14 -> 14; matrix products, arithmetic and copies ran while one was open for 6% -> 11% of each run, Pallas kernels for 0% -> 0%
where the time goes in v1:
time: 365 us; the launch traced here: 357 us
  other arithmetic  175 us (48%)
  waiting for transfers between devices  73.3 us (20%)
  local copies, waits for them, and re-layouts  65.3 us (18%)
  starting transfers between devices  23.7 us (6%)
  between operations  11.2 us (3%)
  loops' own time  9.14 us (3%)
    add x4, other arithmetic, advance(): return centre + change + rate * centre / (1.0 + centre * centre)  59.7 us
    select_n x11, other arithmetic, fourth_pass(): jnp.where(depth_fourth == level, values + factor * (ahead + behind), values)  51.8 us
    ppermute x2, waiting for transfers between devices, local(): lax.ppermute(going_up, 'comp', [(d, (d + 1) % ways) for d in range(ways)])  51.5 us
    select_n x11, other arithmetic, third_pass(): jnp.where(depth_third == level, values + factor * (ahead + behind), values)  25.5 us
    add x4, other arithmetic, add_grid(): inner + jnp.where(found, jnp.take(remote, source, axis=-1), 0.0)  15.4 us
    ppermute x8, starting transfers between devices, extended(): lax.ppermute(lax.slice_in_dim(block, 0, width, axis=dim), axis, backward)  14.8 us
    squeeze x4, local copies, waits for them, and re-layouts, local(): carry, unused = lax.scan(add_grid, carry, (piece, sources))  12.1 us
    ppermute x8, waiting for transfers between devices, extended(): lax.ppermute(lax.slice_in_dim(block, block.shape[dim] - width, None, axis...  11.9 us
  transfers between devices with their start and end apart: 19, of which 14 were waited for; matrix products, arithmetic and copies ran while one was open for 11% of the time, Pallas kernels for 0%

profile of v1, /device:TPU:0, one launch (start us, length us, event | category | flops | bytes accessed | tf_op | source)
XLA Modules:
  0.0 357.4 jit_solution(13435996965488043734)
XLA Ops:
  3.7 5.1 %fusion.316 = (f32[128,16,255]{2,1,0:T(8,128)}, f32[128,16,255]{2,1,0:T(8,128)}) fusion(f32[128,16,256]{2,1,0:T(8,128)} %bitcast.52), kind=kLoop, calls=%fused_computation.727 | loop fusion | bytes 8355840 | tf_op jit(solution)/shard_map/jit(_roll_static)/slice | solution.py:81
  36.4 15.5 %fusion.255 = f32[128,16,256]{2,1,0:T(8,128)S(1)} fusion(f32[128,16,256]{2,1,0:T(8,128)S(1)} %bitcast.55, s32[]{:T(128)S(6)} %select_n.1257, s32[]{:T(128)S(6)} %select_n.1261, f32[1,16,256]{2,1,0:T(8,128)} %copy-done.4, f32[130,1,256]{2,1,0:T(1,128)} %collective-permute-done.3, f32[1,16,256]{2,1,0:T(8,128)} %copy-done.5, ...), kind=kLoop, calls=%fused_computation.526 | loop fusion | flops 26214400 | bytes 8688180 | tf_op jit(solution)/shard_map/add | solution.py:159
  63.8 4.7 %collective-permute-done.7 = f32[130,1,256]{2,1,0:T(1,128)S(1)} collective-permute-done((f32[130,1,256]{2,1,0:T(1,128)S(1)}, f32[130,1,256]{2,1,0:T(1,128)S(1)}, u32[]{:S(2)}, u32[]{:S(2)}) %collective-permute-start.7) | collective-permute-done | bytes 133152 | tf_op jit(solution)/shard_map/ppermute | solution.py:17
  68.5 14.7 %fusion.230 = f32[128,16,256]{2,1,0:T(8,128)S(1)} fusion(f32[128,16,256]{2,1,0:T(8,128)S(1)} %fusion.255, s32[]{:T(128)S(6)} %select_n.1257, s32[]{:T(128)S(6)} %select_n.1261, f32[1,16,256]{2,1,0:T(8,128)S(1)} %collective-permute-done.4, f32[130,1,256]{2,1,0:T(1,128)S(1)} %collective-permute-done.7, f32[1,16,256]{2,1,0:T(8,128)S(1)} %collective-permute-done.5, ...), kind=kLoop, calls=%fused_computation.499 | loop fusion | flops 26214400 | bytes 8688180 | tf_op jit(solution)/shard_map/add | solution.py:159
  94.7 14.7 %fusion.205 = f32[128,16,256]{2,1,0:T(8,128)S(1)} fusion(f32[128,16,256]{2,1,0:T(8,128)S(1)} %fusion.230, s32[]{:T(128)S(6)} %select_n.1257, s32[]{:T(128)S(6)} %select_n.1261, f32[1,16,256]{2,1,0:T(8,128)S(1)} %collective-permute-done.8, f32[130,1,256]{2,1,0:T(1,128)S(1)} %collective-permute-done.11, f32[1,16,256]{2,1,0:T(8,128)S(1)} %collective-permute-done.9, ...), kind=kLoop, calls=%fused_computation.472 | loop fusion | flops 26214400 | bytes 8688180 | tf_op jit(solution)/shard_map/add | solution.py:159
  121.8 14.9 %fusion.180 = f32[128,16,256]{2,1,0:T(8,128)S(1)} fusion(f32[128,16,256]{2,1,0:T(8,128)S(1)} %fusion.205, s32[]{:T(128)S(6)} %select_n.1257, s32[]{:T(128)S(6)} %select_n.1261, f32[1,16,256]{2,1,0:T(8,128)S(1)} %collective-permute-done.12, f32[130,1,256]{2,1,0:T(1,128)S(1)} %collective-permute-done.15, f32[1,16,256]{2,1,0:T(8,128)S(1)} %collective-permute-done.13, ...), kind=kLoop, calls=%fused_computation.445 | loop fusion | flops 26214400 | bytes 8688180 | tf_op jit(solution)/shard_map/add | solution.py:159
  136.7 4.6 %add_select_fusion.23 = f32[128,16,256]{2,1,0:T(8,128)S(1)} fusion(f32[128,16,256]{2,1,0:T(8,128)S(1)} %fusion.180, s32[]{:T(128)S(6)} %select_n.1295, s32[]{:T(128)S(6)} %select_n.1289, s32[]{:T(128)S(6)} %select_n.1291, s32[]{:T(128)S(6)} %select_n.1293, pred[256]{0:T(512)(128)(4,1)S(1)} %copy-done.12, pred[256]{0:T(512)(128)(4,1)S(1)} %copy-done.13, ...), kind=kLoop, calls=%fused_computation.286 | loop fusion | flops 5242880 | bytes 4195088 | tf_op jit(solution)/shard_map/jit(_where)/select_n | solution.py:98
  141.4 4.6 %add_select_fusion.22 = f32[128,16,256]{2,1,0:T(8,128)S(1)} fusion(f32[128,16,256]{2,1,0:T(8,128)S(1)} %add_select_fusion.23, s32[]{:T(128)S(6)} %select_n.1303, s32[]{:T(128)S(6)} %select_n.1297, s32[]{:T(128)S(6)} %select_n.1299, s32[]{:T(128)S(6)} %select_n.1301, pred[256]{0:T(512)(128)(4,1)S(1)} %copy-done.17, pred[256]{0:T(512)(128)(4,1)S(1)} %copy-done.18, ...), kind=kLoop, calls=%fused_computation.285 | loop fusion | flops 5242880 | bytes 4195088 | tf_op jit(solution)/shard_map/jit(_where)/select_n | solution.py:98
  146.1 4.8 %add_select_fusion.21 = f32[128,16,256]{2,1,0:T(8,128)S(1)} fusion(f32[128,16,256]{2,1,0:T(8,128)S(1)} %add_select_fusion.22, s32[]{:T(128)S(6)} %select_n.1311, s32[]{:T(128)S(6)} %select_n.1305, s32[]{:T(128)S(6)} %select_n.1307, s32[]{:T(128)S(6)} %select_n.1309, pred[256]{0:T(512)(128)(4,1)S(1)} %copy-done.21, pred[256]{0:T(512)(128)(4,1)S(1)} %copy-done.22, ...), kind=kLoop, calls=%fused_computation.284 | loop fusion | flops 5242880 | bytes 4195088 | tf_op jit(solution)/shard_map/jit(_where)/select_n | solution.py:98
  151.0 4.6 %add_select_fusion.20 = f32[128,16,256]{2,1,0:T(8,128)S(1)} fusion(f32[128,16,256]{2,1,0:T(8,128)S(1)} %add_select_fusion.21, s32[]{:T(128)S(6)} %select_n.1319, s32[]{:T(128)S(6)} %select_n.1313, s32[]{:T(128)S(6)} %select_n.1315, s32[]{:T(128)S(6)} %select_n.1317, pred[256]{0:T(512)(128)(4,1)S(1)} %copy-done.23, pred[256]{0:T(512)(128)(4,1)S(1)} %copy-done.24, ...), kind=kLoop, calls=%fused_computation.283 | loop fusion | flops 5242880 | bytes 4195088 | tf_op jit(solution)/shard_map/jit(_where)/select_n | solution.py:98
  155.6 4.6 %add_select_fusion.19 = f32[128,16,256]{2,1,0:T(8,128)S(1)} fusion(f32[128,16,256]{2,1,0:T(8,128)S(1)} %add_select_fusion.20, s32[]{:T(128)S(6)} %select_n.1327, s32[]{:T(128)S(6)} %select_n.1321, s32[]{:T(128)S(6)} %select_n.1323, s32[]{:T(128)S(6)} %select_n.1325, pred[256]{0:T(512)(128)(4,1)S(1)} %copy-done.25, pred[256]{0:T(512)(128)(4,1)S(1)} %copy-done.26, ...), kind=kLoop, calls=%fused_computation.282 | loop fusion | flops 5242880 | bytes 4195088 | tf_op jit(solution)/shard_map/jit(_where)/select_n | solution.py:98
  160.3 5.0 %add_select_fusion.18 = f32[128,16,256]{2,1,0:T(8,128)S(1)} fusion(f32[128,16,256]{2,1,0:T(8,128)S(1)} %add_select_fusion.19, s32[]{:T(128)S(6)} %select_n.1335, s32[]{:T(128)S(6)} %select_n.1329, s32[]{:T(128)S(6)} %select_n.1331, s32[]{:T(128)S(6)} %select_n.1333, pred[256]{0:T(512)(128)(4,1)S(1)} %copy-done.29, pred[256]{0:T(512)(128)(4,1)S(1)} %copy-done.30, ...), kind=kLoop, calls=%fused_computation.281 | loop fusion | flops 5242880 | bytes 4195088 | tf_op jit(solution)/shard_map/jit(_where)/select_n | solution.py:98
  181.1 44.5 %collective-permute-done.16 = f32[1,128,16,256]{3,2,1,0:T(8,128)} collective-permute-done((f32[1,128,16,256]{3,2,1,0:T(8,128)S(1)}, f32[1,128,16,256]{3,2,1,0:T(8,128)}, u32[]{:S(2)}, u32[]{:S(2)}) %collective-permute-start.16) | collective-permute-done | bytes 2097184 | tf_op jit(solution)/shard_map/ppermute | solution.py:185
  244.3 7.0 %collective-permute-done.18 = f32[1,128,16,256]{3,2,1,0:T(8,128)} collective-permute-done((f32[1,128,16,256]{3,2,1,0:T(8,128)}, f32[1,128,16,256]{3,2,1,0:T(8,128)}, u32[]{:S(2)}, u32[]{:S(2)}) %collective-permute-start.18) | collective-permute-done | bytes 2097184 | tf_op jit(solution)/shard_map/ppermute | solution.py:185
  255.4 56.1 %while.15 = (s32[]{:T(128)}, f32[128,16,256]{0,1,2:T(8,128)}, s32[4]{0:T(128)S(1)}, s32[4]{0:T(128)S(1)}, s32[256]{0:T(256)S(1)}, /*index=5*/f32[4,128,16,256]{1...) while((s32[]{:T(128)}, f32[128,16,256]{0,1,2:T(8,128)}, ...), condition=%wide.region_5.7_spmd.clone.clone, body=%wide.region_1.6_spmd.sunk.clone.clone.sunk | while | flops 2568969 | bytes 14700981 | solution.py:206
  278.4 4.2 %bitcast_add_fusion.2 = f32[128,16,256]{0,1,2:T(8,128)} fusion(f32[128,16,256]{0,1,2:T(8,128)} %get-tuple-element.350, f32[256,128,16]{1,2,0:T(8,128)S(1)} %gather_fusion, pred[256]{0:T(512)(128)(4,1)S(1)} %compare_reduce_fusion.2, pred[256]{0:T(512)(128)(4,1)S(1)} %compare_and_fusion.2, pred[]{:T(512)S(6)} %compare.119), kind=kLoop, calls=%fused_computation.2.clone.1 | loop fusion | flops 2097152 | bytes 6291969 | tf_op jit(solution)/shard_map/while/body/eval_jaxpr/add | solution.py:203
  292.8 4.2 %bitcast_add_fusion.2 = f32[128,16,256]{0,1,2:T(8,128)} fusion(f32[128,16,256]{0,1,2:T(8,128)} %get-tuple-element.350, f32[256,128,16]{1,2,0:T(8,128)S(1)} %gather_fusion, pred[256]{0:T(512)(128)(4,1)S(1)} %compare_reduce_fusion.2, pred[256]{0:T(512)(128)(4,1)S(1)} %compare_and_fusion.2, pred[]{:T(512)S(6)} %compare.119), kind=kLoop, calls=%fused_computation.2.clone.1 | loop fusion | flops 2097152 | bytes 6291969 | tf_op jit(solution)/shard_map/while/body/eval_jaxpr/add | solution.py:203
  307.2 4.2 %bitcast_add_fusion.2 = f32[128,16,256]{0,1,2:T(8,128)} fusion(f32[128,16,256]{0,1,2:T(8,128)} %get-tuple-element.350, f32[256,128,16]{1,2,0:T(8,128)S(1)} %gather_fusion, pred[256]{0:T(512)(128)(4,1)S(1)} %compare_reduce_fusion.2, pred[256]{0:T(512)(128)(4,1)S(1)} %compare_and_fusion.2, pred[]{:T(512)S(6)} %compare.119), kind=kLoop, calls=%fused_computation.2.clone.1 | loop fusion | flops 2097152 | bytes 6291969 | tf_op jit(solution)/shard_map/while/body/eval_jaxpr/add | solution.py:203
  327.9 4.6 %add_select_fusion.5 = f32[128,16,256]{2,1,0:T(8,128)S(1)} fusion(f32[128,16,256]{2,1,0:T(8,128)S(1)} %add_select_fusion.6, s32[]{:T(128)S(6)} %select_n.1335, s32[]{:T(128)S(6)} %select_n.1329, s32[]{:T(128)S(6)} %select_n.1331, s32[]{:T(128)S(6)} %select_n.1333, pred[256]{0:T(512)(128)(4,1)S(1)} %copy-done.29, pred[256]{0:T(512)(128)(4,1)S(1)} %copy-done.30, ...), kind=kLoop, calls=%fused_computation.268 | loop fusion | flops 5242880 | bytes 4195088 | tf_op jit(solution)/shard_map/jit(_where)/select_n | solution.py:98
  332.5 4.6 %add_select_fusion.4 = f32[128,16,256]{2,1,0:T(8,128)S(1)} fusion(f32[128,16,256]{2,1,0:T(8,128)S(1)} %add_select_fusion.5, s32[]{:T(128)S(6)} %select_n.1327, s32[]{:T(128)S(6)} %select_n.1321, s32[]{:T(128)S(6)} %select_n.1323, s32[]{:T(128)S(6)} %select_n.1325, pred[256]{0:T(512)(128)(4,1)S(1)} %copy-done.25, pred[256]{0:T(512)(128)(4,1)S(1)} %copy-done.26, ...), kind=kLoop, calls=%fused_computation.267 | loop fusion | flops 5242880 | bytes 4195088 | tf_op jit(solution)/shard_map/jit(_where)/select_n | solution.py:98
  337.1 4.8 %add_select_fusion.3 = f32[128,16,256]{2,1,0:T(8,128)S(1)} fusion(f32[128,16,256]{2,1,0:T(8,128)S(1)} %add_select_fusion.4, s32[]{:T(128)S(6)} %select_n.1319, s32[]{:T(128)S(6)} %select_n.1313, s32[]{:T(128)S(6)} %select_n.1315, s32[]{:T(128)S(6)} %select_n.1317, pred[256]{0:T(512)(128)(4,1)S(1)} %copy-done.23, pred[256]{0:T(512)(128)(4,1)S(1)} %copy-done.24, ...), kind=kLoop, calls=%fused_computation.266 | loop fusion | flops 5242880 | bytes 4195088 | tf_op jit(solution)/shard_map/jit(_where)/select_n | solution.py:98
  341.9 4.6 %add_select_fusion.2 = f32[128,16,256]{2,1,0:T(8,128)S(1)} fusion(f32[128,16,256]{2,1,0:T(8,128)S(1)} %add_select_fusion.3, s32[]{:T(128)S(6)} %select_n.1311, s32[]{:T(128)S(6)} %select_n.1305, s32[]{:T(128)S(6)} %select_n.1307, s32[]{:T(128)S(6)} %select_n.1309, pred[256]{0:T(512)(128)(4,1)S(1)} %copy-done.21, pred[256]{0:T(512)(128)(4,1)S(1)} %copy-done.22, ...), kind=kLoop, calls=%fused_computation.265 | loop fusion | flops 5242880 | bytes 4195088 | tf_op jit(solution)/shard_map/jit(_where)/select_n | solution.py:98
  346.6 4.8 %add_select_fusion.1 = f32[128,16,256]{2,1,0:T(8,128)S(1)} fusion(f32[128,16,256]{2,1,0:T(8,128)S(1)} %add_select_fusion.2, s32[]{:T(128)S(6)} %select_n.1303, s32[]{:T(128)S(6)} %select_n.1297, s32[]{:T(128)S(6)} %select_n.1299, s32[]{:T(128)S(6)} %select_n.1301, pred[256]{0:T(512)(128)(4,1)S(1)} %copy-done.17, pred[256]{0:T(512)(128)(4,1)S(1)} %copy-done.18, ...), kind=kLoop, calls=%fused_computation.264 | loop fusion | flops 5242880 | bytes 4195088 | tf_op jit(solution)/shard_map/jit(_where)/select_n | solution.py:98
  351.4 5.8 %fusion.24 = f32[1,128,16,256]{3,2,1,0:T(8,128)} fusion(f32[128,16,256]{2,1,0:T(8,128)S(1)} %add_select_fusion.1, s32[]{:T(128)S(6)} %select_n.1295, s32[]{:T(128)S(6)} %select_n.1289, s32[]{:T(128)S(6)} %select_n.1291, s32[]{:T(128)S(6)} %select_n.1293, pred[256]{0:T(512)(128)(4,1)S(1)} %copy-done.12, pred[256]{0:T(512)(128)(4,1)S(1)} %copy-done.13, ...), kind=kLoop, calls=%fused_computation.289 | loop fusion | flops 5242880 | bytes 4195088 | tf_op jit(solution)/shard_map/broadcast_in_dim | solution.py:207
  (217 shorter events, 145.8 us)
Async XLA Ops:
  0.7 22.6 %collective-permute-start = (f32[1,16,256]{2,1,0:T(8,128)S(1)}, f32[1,16,256]{2,1,0:T(8,128)S(1)}, u32[]{:S(2)}, u32[]{:S(2)}) collective-permute-start(f32[1,16,256]{2,1,0:T(8,128)S(1)} %get-tuple-element.260), channel_id=1, source_target_pairs={{4,0},{0,4},{5,1},{1,5},{6,2},{2,6},{7,3},{3,7},{12,8},{8,12},{13,... | collective-permute-start | bytes 49160 | tf_op jit(solution)/shard_map/ppermute | solution.py:20
  3.7 19.7 %collective-permute-start.1 = (f32[1,16,256]{2,1,0:T(8,128)S(1)}, f32[1,16,256]{2,1,0:T(8,128)S(1)}, u32[]{:S(2)}, u32[]{:S(2)}) collective-permute-start(f32[1,16,256]{2,1,0:T(8,128)S(1)} %get-tuple-element.259), channel_id=1, source_target_pairs={{0,4},{4,0},{1,5},{5,1},{2,6},{6,2},{3,7},{7,3},{8,12},{12,8},{9,1... | collective-permute-start | bytes 49160 | tf_op jit(solution)/shard_map/ppermute | solution.py:17
  24.0 12.4 %collective-permute-start.2 = (f32[130,1,256]{2,1,0:T(1,128)S(1)}, f32[130,1,256]{2,1,0:T(1,128)S(1)}, u32[]{:S(2)}, u32[]{:S(2)}) collective-permute-start(f32[130,1,256]{2,1,0:T(1,128)S(1)} %get-tuple-element.235), channel_id=1, source_target_pairs={{1,0},{2,1},{3,2},{0,3},{5,4},{6,5},{7,6},{4,7},{9,8},{10,9},{11,1... | collective-permute-start | bytes 399368 | tf_op jit(solution)/shard_map/ppermute | solution.py:20
  28.1 8.3 %collective-permute-start.3 = (f32[130,1,256]{2,1,0:T(1,128)S(1)}, f32[130,1,256]{2,1,0:T(1,128)}, u32[]{:S(2)}, u32[]{:S(2)}) collective-permute-start(f32[130,1,256]{2,1,0:T(1,128)S(1)} %get-tuple-element.236), channel_id=1, source_target_pairs={{0,1},{1,2},{2,3},{3,0},{4,5},{5,6},{6,7},{7,4},{8,9},{9,10},{10,1... | collective-permute-start | bytes 399368 | tf_op jit(solution)/shard_map/ppermute | solution.py:17
  51.9 3.8 %collective-permute-start.4 = (f32[1,16,256]{2,1,0:T(8,128)S(1)}, f32[1,16,256]{2,1,0:T(8,128)S(1)}, u32[]{:S(2)}, u32[]{:S(2)}) collective-permute-start(f32[1,16,256]{2,1,0:T(8,128)S(1)} %get-tuple-element.254), channel_id=1, source_target_pairs={{4,0},{0,4},{5,1},{1,5},{6,2},{2,6},{7,3},{3,7},{12,8},{8,12},{13,... | collective-permute-start | bytes 49160 | tf_op jit(solution)/shard_map/ppermute | solution.py:20
  53.5 3.7 %collective-permute-start.5 = (f32[1,16,256]{2,1,0:T(8,128)S(1)}, f32[1,16,256]{2,1,0:T(8,128)S(1)}, u32[]{:S(2)}, u32[]{:S(2)}) collective-permute-start(f32[1,16,256]{2,1,0:T(8,128)S(1)} %get-tuple-element.253), channel_id=1, source_target_pairs={{0,4},{4,0},{1,5},{5,1},{2,6},{6,2},{3,7},{7,3},{8,12},{12,8},{9,1... | collective-permute-start | bytes 49160 | tf_op jit(solution)/shard_map/ppermute | solution.py:17
  57.4 6.4 %collective-permute-start.6 = (f32[130,1,256]{2,1,0:T(1,128)S(1)}, f32[130,1,256]{2,1,0:T(1,128)S(1)}, u32[]{:S(2)}, u32[]{:S(2)}) collective-permute-start(f32[130,1,256]{2,1,0:T(1,128)S(1)} %get-tuple-element.233), channel_id=1, source_target_pairs={{1,0},{2,1},{3,2},{0,3},{5,4},{6,5},{7,6},{4,7},{9,8},{10,9},{11,1... | collective-permute-start | bytes 399368 | tf_op jit(solution)/shard_map/ppermute | solution.py:20
  61.3 7.2 %collective-permute-start.7 = (f32[130,1,256]{2,1,0:T(1,128)S(1)}, f32[130,1,256]{2,1,0:T(1,128)S(1)}, u32[]{:S(2)}, u32[]{:S(2)}) collective-permute-start(f32[130,1,256]{2,1,0:T(1,128)S(1)} %get-tuple-element.234), channel_id=1, source_target_pairs={{0,1},{1,2},{2,3},{3,0},{4,5},{5,6},{6,7},{7,4},{8,9},{9,10},{10,1... | collective-permute-start | bytes 399368 | tf_op jit(solution)/shard_map/ppermute | solution.py:17
  83.2 3.8 %collective-permute-start.8 = (f32[1,16,256]{2,1,0:T(8,128)S(1)}, f32[1,16,256]{2,1,0:T(8,128)S(1)}, u32[]{:S(2)}, u32[]{:S(2)}) collective-permute-start(f32[1,16,256]{2,1,0:T(8,128)S(1)} %get-tuple-element.248), channel_id=1, source_target_pairs={{4,0},{0,4},{5,1},{1,5},{6,2},{2,6},{7,3},{3,7},{12,8},{8,12},{13,... | collective-permute-start | bytes 49160 | tf_op jit(solution)/shard_map/ppermute | solution.py:20
  83.8 3.7 %collective-permute-start.9 = (f32[1,16,256]{2,1,0:T(8,128)S(1)}, f32[1,16,256]{2,1,0:T(8,128)S(1)}, u32[]{:S(2)}, u32[]{:S(2)}) collective-permute-start(f32[1,16,256]{2,1,0:T(8,128)S(1)} %get-tuple-element.247), channel_id=1, source_target_pairs={{0,4},{4,0},{1,5},{5,1},{2,6},{6,2},{3,7},{7,3},{8,12},{12,8},{9,1... | collective-permute-start | bytes 49160 | tf_op jit(solution)/shard_map/ppermute | solution.py:17
  87.8 5.0 %collective-permute-start.10 = (f32[130,1,256]{2,1,0:T(1,128)S(1)}, f32[130,1,256]{2,1,0:T(1,128)S(1)}, u32[]{:S(2)}, u32[]{:S(2)}) collective-permute-start(f32[130,1,256]{2,1,0:T(1,128)S(1)} %get-tuple-element.231), channel_id=1, source_target_pairs={{1,0},{2,1},{3,2},{0,3},{5,4},{6,5},{7,6},{4,7},{9,8},{10,9},{11,1... | collective-permute-start | bytes 399368 | tf_op jit(solution)/shard_map/ppermute | solution.py:20
  87.8 6.8 %collective-permute-start.11 = (f32[130,1,256]{2,1,0:T(1,128)S(1)}, f32[130,1,256]{2,1,0:T(1,128)S(1)}, u32[]{:S(2)}, u32[]{:S(2)}) collective-permute-start(f32[130,1,256]{2,1,0:T(1,128)S(1)} %get-tuple-element.232), channel_id=1, source_target_pairs={{0,1},{1,2},{2,3},{3,0},{4,5},{5,6},{6,7},{7,4},{8,9},{9,10},{10,1... | collective-permute-start | bytes 399368 | tf_op jit(solution)/shard_map/ppermute | solution.py:17
  109.4 3.8 %collective-permute-start.12 = (f32[1,16,256]{2,1,0:T(8,128)S(1)}, f32[1,16,256]{2,1,0:T(8,128)S(1)}, u32[]{:S(2)}, u32[]{:S(2)}) collective-permute-start(f32[1,16,256]{2,1,0:T(8,128)S(1)} %get-tuple-element.242), channel_id=1, source_target_pairs={{4,0},{0,4},{5,1},{1,5},{6,2},{2,6},{7,3},{3,7},{12,8},{8,12},{13,... | collective-permute-start | bytes 49160 | tf_op jit(solution)/shard_map/ppermute | solution.py:20
  110.9 3.7 %collective-permute-start.13 = (f32[1,16,256]{2,1,0:T(8,128)S(1)}, f32[1,16,256]{2,1,0:T(8,128)S(1)}, u32[]{:S(2)}, u32[]{:S(2)}) collective-permute-start(f32[1,16,256]{2,1,0:T(8,128)S(1)} %get-tuple-element.241), channel_id=1, source_target_pairs={{0,4},{4,0},{1,5},{5,1},{2,6},{6,2},{3,7},{7,3},{8,12},{12,8},{9,1... | collective-permute-start | bytes 49160 | tf_op jit(solution)/shard_map/ppermute | solution.py:17
  114.9 5.0 %collective-permute-start.14 = (f32[130,1,256]{2,1,0:T(1,128)S(1)}, f32[130,1,256]{2,1,0:T(1,128)S(1)}, u32[]{:S(2)}, u32[]{:S(2)}) collective-permute-start(f32[130,1,256]{2,1,0:T(1,128)S(1)} %get-tuple-element.229), channel_id=1, source_target_pairs={{1,0},{2,1},{3,2},{0,3},{5,4},{6,5},{7,6},{4,7},{9,8},{10,9},{11,1... | collective-permute-start | bytes 399368 | tf_op jit(solution)/shard_map/ppermute | solution.py:20
  114.9 6.8 %collective-permute-start.15 = (f32[130,1,256]{2,1,0:T(1,128)S(1)}, f32[130,1,256]{2,1,0:T(1,128)S(1)}, u32[]{:S(2)}, u32[]{:S(2)}) collective-permute-start(f32[130,1,256]{2,1,0:T(1,128)S(1)} %get-tuple-element.230), channel_id=1, source_target_pairs={{0,1},{1,2},{2,3},{3,0},{4,5},{5,6},{6,7},{7,4},{8,9},{9,10},{10,1... | collective-permute-start | bytes 399368 | tf_op jit(solution)/shard_map/ppermute | solution.py:17
  121.8 14.9 %copy-start.11 = (pred[256]{0:T(512)(128)(4,1)S(1)}, pred[256]{0:T(512)(128)(4,1)}, u32[]{:S(2)}) copy-start(pred[256]{0:T(512)(128)(4,1)} %get-tuple-element.272) | copy-start | bytes 772
  121.8 14.9 %copy-start.12 = (pred[256]{0:T(512)(128)(4,1)S(1)}, pred[256]{0:T(512)(128)(4,1)}, u32[]{:S(2)}) copy-start(pred[256]{0:T(512)(128)(4,1)} %get-tuple-element.291) | copy-start | bytes 772
  121.8 14.9 %copy-start.13 = (pred[256]{0:T(512)(128)(4,1)S(1)}, pred[256]{0:T(512)(128)(4,1)}, u32[]{:S(2)}) copy-start(pred[256]{0:T(512)(128)(4,1)} %get-tuple-element.292) | copy-start | bytes 772
  177.0 48.6 %copy-start.10 = (s32[256]{0:T(256)S(1)}, s32[256]{0:T(256)}, u32[]{:S(2)}) copy-start(s32[256]{0:T(256)} %copy-done.9) | copy-start | bytes 3076
  177.0 48.6 %copy-start.6 = (s32[49]{0:T(128)S(1)}, s32[49]{0:T(128)}, u32[]{:S(2)}) copy-start(s32[49]{0:T(128)} %constant.625.clone) | copy-start | bytes 592
  179.3 46.3 %collective-permute-start.16 = (f32[1,128,16,256]{3,2,1,0:T(8,128)S(1)}, f32[1,128,16,256]{3,2,1,0:T(8,128)}, u32[]{:S(2)}, u32[]{:S(2)}) collective-permute-start(f32[1,128,16,256]{3,2,1,0:T(8,128)S(1)} %fusion.23), channel_id=1, source_target_pairs={{0,8},{8,16},{16,24},{24,0},{1,9},{9,17},{17,25},{25,1},{2,10},{10... | collective-permute-start | bytes 6291464 | tf_op jit(solution)/shard_map/ppermute | solution.py:185
  179.4 57.6 %collective-permute-start.17 = (f32[1,128,16,256]{3,2,1,0:T(8,128)S(1)}, f32[1,128,16,256]{3,2,1,0:T(8,128)}, u32[]{:S(2)}, u32[]{:S(2)}) collective-permute-start(f32[1,128,16,256]{3,2,1,0:T(8,128)S(1)} %fusion.23), channel_id=1, source_target_pairs={{0,24},{8,0},{16,8},{24,16},{1,25},{9,1},{17,9},{25,17},{2,26},{10... | collective-permute-start | bytes 6291464 | tf_op jit(solution)/shard_map/ppermute | solution.py:188
  225.6 25.8 %collective-permute-start.18 = (f32[1,128,16,256]{3,2,1,0:T(8,128)}, f32[1,128,16,256]{3,2,1,0:T(8,128)}, u32[]{:S(2)}, u32[]{:S(2)}) collective-permute-start(f32[1,128,16,256]{3,2,1,0:T(8,128)} %collective-permute-done.16), channel_id=1, source_target_pairs={{0,8},{8,16},{16,24},{24,0},{1,9},{9,17},{17,25},{25,1},{2,10},{10... | collective-permute-start | bytes 6291464 | tf_op jit(solution)/shard_map/ppermute | solution.py:185
  (33 other events, 143.4 us)
